TPU v7x, 32 devices: a whole 2x2x4 slice. The times are simulated.
32 devices in a mesh: groups: 2 (over y), seq: 16 (over z, x, core).
Axes of the slice: x: 2, y: 2, z: 4, core: 2. Of those that a mesh axis runs over, the one named last changes fastest.
Arguments:
- queries: bfloat16 [12288, 2048], P(('groups', 'seq')), parts along dimension 0, may hold values from -6 to 6
- key_vectors: bfloat16 [12288, 2048], P(('groups', 'seq')), parts along dimension 0, may hold values from -6 to 6
- value_vectors: bfloat16 [12288, 2048], P(('groups', 'seq')), parts along dimension 0, may hold values from -6 to 6
- out_cotangent: bfloat16 [12288, 2048], P(('groups', 'seq')), parts along dimension 0, may hold values from -6 to 6
- norm_gain: float32 [2048], replicated, may hold values from 0.1 to 1.9
Outputs:
- query_grad: bfloat16 [12288, 2048], P(('groups', 'seq')), parts along dimension 0
- key_grad: bfloat16 [12288, 2048], P(('groups', 'seq')), parts along dimension 0
- value_grad: bfloat16 [12288, 2048], P(('groups', 'seq')), parts along dimension 0
- gain_grad: float32 [4096], P('groups'), parts along dimension 0
There are 2 independent parts, one for each index of `groups`. A program takes and returns all parts, laid end to end along the dimension named above; an argument that names none is the same for every part. Nothing has to cross between parts.
All inputs are finite; a program needn't handle non-finite values.
Results may differ from a plain program's by a relative error of at most 0.011.
Values may be sent and summed in bfloat16 or wider, within the bound.
No kernel may reach another device: no remote copies, remote signals or barrier semaphores. Data moves between devices by JAX's collectives and lax.ppermute only.
A program may use at most 128 MiB of HBM per device.

v0:
```python
import jax
import jax.numpy as jnp
from jax import lax
from jax.sharding import PartitionSpec as P

HEADS = 16
HEAD = 128
norm_eps = 1e-05


def shifted(value, axis, steps):
    count = lax.axis_size(axis)
    first, last = (max(0, -steps), min(count, count - steps))
    return lax.ppermute(value, axis, [(source, source + steps) for source in range(first, last)])


def feature(x):
    return jnp.where(x > 0, x + 1.0, jnp.exp(jnp.minimum(x, 0.0)))


def slope(x):
    return jnp.where(x > 0, 1.0, jnp.exp(jnp.minimum(x, 0.0)))


def on_device(queries, key_vectors, value_vectors, out_cotangent, norm_gain):
    length = queries.shape[0]
    shards = lax.axis_size("seq")
    rounds = (shards - 1).bit_length()
    query_raw = queries.reshape(length, HEADS, HEAD)
    key_raw = key_vectors.reshape(length, HEADS, HEAD)
    value_rows = value_vectors.reshape(length, HEADS, HEAD)
    cotan = out_cotangent.reshape(length, HEADS, HEAD).astype(jnp.float32)
    query_map = feature(query_raw.astype(jnp.float32)).astype(jnp.bfloat16)
    key_map = feature(key_raw.astype(jnp.float32)).astype(jnp.bfloat16)
    own_state = jnp.einsum("thd,the->hde", key_map, value_rows, preferred_element_type=jnp.float32)
    running = own_state
    for level in range(rounds):
        running = running + shifted(running, "seq", 1 << level)
    state_low = (running - own_state).astype(jnp.bfloat16)
    causal = jnp.tril(jnp.ones((length, length), dtype=bool))[None]
    scores = jnp.einsum("thd,shd->hts", query_map, key_map, preferred_element_type=jnp.float32)
    weights = jnp.where(causal, scores, 0.0).astype(jnp.bfloat16)
    mixed = jnp.einsum("hts,she->the", weights, value_rows, preferred_element_type=jnp.float32)
    mixed = mixed + jnp.einsum(
        "thd,hde->the", query_map, state_low, preferred_element_type=jnp.float32
    )
    rms = jnp.sqrt(jnp.mean(mixed * mixed, axis=-1, keepdims=True) + norm_eps)
    normed = mixed / rms
    gain_part = jnp.sum(cotan * normed, axis=0)
    scaled = cotan * norm_gain.reshape(HEADS, HEAD)
    grad_mixed = (
        (scaled - normed * jnp.mean(scaled * normed, axis=-1, keepdims=True)) / rms
    ).astype(jnp.bfloat16)
    query_state = jnp.einsum(
        "thd,the->hde", query_map, grad_mixed, preferred_element_type=jnp.float32
    )
    later = query_state
    for level in range(rounds):
        later = later + shifted(later, "seq", -(1 << level))
    back_low = (later - query_state).astype(jnp.bfloat16)
    gain_total = lax.psum(gain_part, "seq")
    d_scores = jnp.einsum(
        "the,she->hts", grad_mixed, value_rows, preferred_element_type=jnp.float32
    )
    d_weights = jnp.where(causal, d_scores, 0.0).astype(jnp.bfloat16)
    d_query = jnp.einsum("hts,shd->thd", d_weights, key_map, preferred_element_type=jnp.float32)
    d_query = d_query + jnp.einsum(
        "the,hde->thd", grad_mixed, state_low, preferred_element_type=jnp.float32
    )
    d_key = jnp.einsum("hts,thd->shd", d_weights, query_map, preferred_element_type=jnp.float32)
    d_key = d_key + jnp.einsum(
        "the,hde->thd", value_rows, back_low, preferred_element_type=jnp.float32
    )
    d_value = jnp.einsum("hts,the->she", weights, grad_mixed, preferred_element_type=jnp.float32)
    d_value = d_value + jnp.einsum(
        "thd,hde->the", key_map, back_low, preferred_element_type=jnp.float32
    )
    query_grad = (d_query * slope(query_raw.astype(jnp.float32))).astype(jnp.bfloat16)
    key_grad = (d_key * slope(key_raw.astype(jnp.float32))).astype(jnp.bfloat16)
    value_grad = d_value.astype(jnp.bfloat16)
    flat = (length, HEADS * HEAD)
    return (
        query_grad.reshape(flat),
        key_grad.reshape(flat),
        value_grad.reshape(flat),
        gain_total.reshape(HEADS * HEAD),
    )


def solution(mesh):
    placed = (
        P(("groups", "seq"), None),
        P(("groups", "seq"), None),
        P(("groups", "seq"), None),
        P(("groups", "seq"), None),
        P(),
    )
    return jax.shard_map(
        on_device,
        mesh=mesh,
        in_specs=placed,
        out_specs=(
            P(("groups", "seq"), None),
            P(("groups", "seq"), None),
            P(("groups", "seq"), None),
            P("groups"),
        ),
        check_vma=False,
    )
```

profile of v0, /device:TPU:16, one launch (start us, length us, event | category | flops | bytes accessed | tf_op | source)
XLA Modules:
  0.0 292.3 jit_solution(8299461528966683161)
XLA Ops:
  0.6 4.7 %fusion.3 = (f32[384,2048]{1,0:T(8,128)}, bf16[48,16,8,128]{3,2,1,0:T(8,128)(2,1)}, bf16[48,8,16,128]{3,1,2,0:T(8,128)(2,1)S(1)}) fusion(bf16[384,2048]{1,0:T(8,128)(2,1)} %param.6), kind=kLoop, calls=%fused_computation.11 | loop fusion | flops 5505024 | bytes 7864320 | tf_op jit(solution)/shard_map/jit(_where)/select_n | solution.py:22
  5.3 1.6 copy.40
  6.9 2.1 copy.19
  9.0 0.6 fusion.14
  9.6 1.9 collective-permute-start
  11.5 15.1 %collective-permute-done = f32[16,128,128]{2,1,0:T(8,128)S(1)} collective-permute-done((f32[16,128,128]{2,1,0:T(8,128)S(1)}, f32[16,128,128]{2,1,0:T(8,128)S(1)}, u32[]{:S(2)}, u32[]{:S(2)}) %collective-permute-start) | collective-permute-done | bytes 1048608 | tf_op jit(solution)/shard_map/ppermute | solution.py:14
  26.8 2.5 collective-permute-start.1
  29.3 23.6 %collective-permute-done.1 = f32[16,128,128]{2,1,0:T(8,128)S(1)} collective-permute-done((f32[16,128,128]{2,1,0:T(8,128)S(1)}, f32[16,128,128]{2,1,0:T(8,128)S(1)}, u32[]{:S(2)}, u32[]{:S(2)}) %collective-permute-start.1) | collective-permute-done | bytes 1048608 | tf_op jit(solution)/shard_map/ppermute | solution.py:14
  53.0 3.6 %collective-permute-start.2 = (f32[16,128,128]{2,1,0:T(8,128)S(1)}, f32[16,128,128]{2,1,0:T(8,128)S(1)}, u32[]{:S(2)}, u32[]{:S(2)}) collective-permute-start(f32[16,128,128]{2,1,0:T(8,128)S(1)} %add.67), channel_id=1, source_target_pairs={{0,4},{1,5},{2,6},{3,7},{4,8},{5,9},{6,10},{7,11},{8,12},{9,13},{1... | collective-permute-start | bytes 3145736 | tf_op jit(solution)/shard_map/ppermute | solution.py:14
  56.7 20.8 %collective-permute-done.2 = f32[16,128,128]{2,1,0:T(8,128)S(1)} collective-permute-done((f32[16,128,128]{2,1,0:T(8,128)S(1)}, f32[16,128,128]{2,1,0:T(8,128)S(1)}, u32[]{:S(2)}, u32[]{:S(2)}) %collective-permute-start.2) | collective-permute-done | bytes 1048608 | tf_op jit(solution)/shard_map/ppermute | solution.py:14
  77.4 1.1 add.68
  78.6 1.4 collective-permute-start.3
  80.0 3.1 %fusion.5 = (bf16[384,2048]{1,0:T(8,128)(2,1)}, f32[384,2048]{1,0:T(8,128)}) fusion(bf16[384,2048]{1,0:T(8,128)(2,1)S(1)} %copy-done.17), kind=kLoop, calls=%fused_computation.13 | loop fusion | flops 5505024 | bytes 6291456 | tf_op jit(solution)/shard_map/convert.1
  83.0 2.1 copy.9
  85.2 1.9 copy.37
  87.1 3.1 %select_convert_fusion.1 = bf16[16,384,384]{2,1,0:T(8,128)(2,1)S(1)} fusion(pred[384,384]{1,0:T(8,128)(4,1)S(1)} %iota_compare_fusion, bf16[384,16,128]{0,2,1:T(8,128)(2,1)S(1)} %bitcast.76, bf16[48,16,8,128]{3,2,1,0:T(8,128)(2,1)} %get-tuple-element.11), kind=kOutput, calls=%fused_computation.1 | convolution fusion | flops 608698368 | bytes 8011776 | tf_op jit(solution)/shard_map/thd,shd->hts/dot_general | solution.py:41
  90.2 1.6 fusion.10
  92.3 11.0 %collective-permute-done.3 = f32[16,128,128]{2,1,0:T(8,128)} collective-permute-done((f32[16,128,128]{2,1,0:T(8,128)}, f32[16,128,128]{2,1,0:T(8,128)}, u32[]{:S(2)}, u32[]{:S(2)}) %collective-permute-start.3) | collective-permute-done | bytes 1048608 | tf_op jit(solution)/shard_map/ppermute | solution.py:14
  103.3 1.8 subtract_convert_fusion.1
  105.1 0.7 multiply_reduce_fusion.2
  105.9 1.3 copy-done.1
  107.2 1.3 multiply_reduce_fusion
  108.5 0.8 divide_convert_fusion
  109.3 0.8 fusion.28
  110.1 23.0 %collective-permute-start.4 = (f32[16,128,128]{2,1,0:T(8,128)S(1)}, f32[16,128,128]{2,1,0:T(8,128)S(1)}, u32[]{:S(2)}, u32[]{:S(2)}) collective-permute-start(f32[16,128,128]{2,1,0:T(8,128)S(1)} %fusion.28), channel_id=1, source_target_pairs={{1,0},{2,1},{3,2},{4,3},{5,4},{6,5},{7,6},{8,7},{9,8},{10,9},{11,1... | collective-permute-start | bytes 3145736 | tf_op jit(solution)/shard_map/ppermute | solution.py:14
  133.1 12.3 %collective-permute-done.4 = f32[16,128,128]{2,1,0:T(8,128)S(1)} collective-permute-done((f32[16,128,128]{2,1,0:T(8,128)S(1)}, f32[16,128,128]{2,1,0:T(8,128)S(1)}, u32[]{:S(2)}, u32[]{:S(2)}) %collective-permute-start.4) | collective-permute-done | bytes 1048608 | tf_op jit(solution)/shard_map/ppermute | solution.py:14
  145.6 3.8 %collective-permute-start.5 = (f32[16,128,128]{2,1,0:T(8,128)S(1)}, f32[16,128,128]{2,1,0:T(8,128)S(1)}, u32[]{:S(2)}, u32[]{:S(2)}) collective-permute-start(f32[16,128,128]{2,1,0:T(8,128)S(1)} %add.75), channel_id=1, source_target_pairs={{2,0},{3,1},{4,2},{5,3},{6,4},{7,5},{8,6},{9,7},{10,8},{11,9},{12,... | collective-permute-start | bytes 3145736 | tf_op jit(solution)/shard_map/ppermute | solution.py:14
  149.4 23.2 %collective-permute-done.5 = f32[16,128,128]{2,1,0:T(8,128)S(1)} collective-permute-done((f32[16,128,128]{2,1,0:T(8,128)S(1)}, f32[16,128,128]{2,1,0:T(8,128)S(1)}, u32[]{:S(2)}, u32[]{:S(2)}) %collective-permute-start.5) | collective-permute-done | bytes 1048608 | tf_op jit(solution)/shard_map/ppermute | solution.py:14
  172.7 1.1 add.76
  173.7 2.9 collective-permute-start.6
  176.6 3.5 %copy.21 = f32[384,2048]{0,1:T(8,128)} copy(f32[384,2048]{1,0:T(8,128)} %get-tuple-element.14) | data formatting | bytes 6291456 | tf_op jit(solution)/shard_map/jit(_where)/select_n | solution.py:22
  180.1 3.5 %copy.26 = f32[384,2048]{0,1:T(8,128)} copy(f32[384,2048]{1,0:T(8,128)} %get-tuple-element.10) | data formatting | bytes 6291456 | tf_op jit(solution)/shard_map/jit(_where)/select_n | solution.py:22
  183.7 3.2 %select_convert_fusion = bf16[16,384,384]{2,1,0:T(8,128)(2,1)S(1)} fusion(pred[384,384]{1,0:T(8,128)(4,1)S(1)} %iota_compare_fusion, bf16[384,16,128]{0,2,1:T(8,128)(2,1)} %copy-done.2, bf16[384,2048]{1,0:T(8,128)(2,1)S(1)} %copy-done), kind=kOutput, calls=%fused_computation | convolution fusion | flops 608698368 | bytes 8011776 | tf_op jit(solution)/shard_map/the,she->hts/dot_general | solution.py:62
  186.9 1.6 fusion.26
  188.5 0.8 copy-done.5
  189.3 12.7 %collective-permute-done.6 = f32[16,128,128]{2,1,0:T(8,128)} collective-permute-done((f32[16,128,128]{2,1,0:T(8,128)}, f32[16,128,128]{2,1,0:T(8,128)}, u32[]{:S(2)}, u32[]{:S(2)}) %collective-permute-start.6) | collective-permute-done | bytes 1048608 | tf_op jit(solution)/shard_map/ppermute | solution.py:14
  202.0 2.6 add.77
  204.6 3.1 %collective-permute-start.7 = (f32[16,128,128]{2,1,0:T(8,128)}, f32[16,128,128]{2,1,0:T(8,128)}, u32[]{:S(2)}, u32[]{:S(2)}) collective-permute-start(f32[16,128,128]{2,1,0:T(8,128)} %add.77), channel_id=1, source_target_pairs={{8,0},{9,1},{10,2},{11,3},{12,4},{13,5},{14,6},{15,7},{24,16},{25,... | collective-permute-start | bytes 3145736 | tf_op jit(solution)/shard_map/ppermute | solution.py:14
  207.7 2.0 fusion.9
  209.6 2.6 copy.29
  212.2 60.8 %psum.7 = f32[2048]{0:T(1024)} all-reduce(f32[2048]{0:T(1024)S(1)} %bitcast.88), channel_id=1, replica_groups=mesh['groups'=2,'seq'=16] {'seq'}, use_global_device_ids=true, to_apply=%region_3.4 | all-reduce | flops 2048 | bytes 16384 | tf_op jit(solution)/shard_map/psum | solution.py:61
  273.1 4.0 %fusion.29 = f32[16,128,384]{2,1,0:T(8,128)S(1)} fusion(bf16[384,16,128]{0,2,1:T(8,128)(2,1)} %copy-done.2, bf16[16,384,384]{2,1,0:T(8,128)(2,1)} %copy-done.4), kind=kOutput, calls=%fused_computation.51 | convolution fusion | flops 603979776 | bytes 9437184 | tf_op jit(solution)/shard_map/hts,the->she/dot_general | solution.py:74
  277.1 5.3 %fusion.27 = f32[16,128,384]{2,1,0:T(8,128)} fusion(bf16[384,16,128]{0,2,1:T(8,128)(2,1)S(1)} %bitcast.79, bf16[16,384,384]{2,1,0:T(8,128)(2,1)} %copy-done.5), kind=kOutput, calls=%fused_computation.49 | convolution fusion | flops 603979776 | bytes 9437184 | tf_op jit(solution)/shard_map/hts,thd->shd/dot_general | solution.py:70
  282.4 1.9 subtract_convert_fusion
  284.5 0.8 add_convert_fusion
  285.3 1.6 copy.31
  286.9 3.8 %fusion.8 = bf16[384,16,128]{0,2,1:T(8,128)(2,1)S(1)} fusion(f32[384,16,128]{0,2,1:T(8,128)} %bitcast.80, f32[16,128,384]{2,1,0:T(8,128)} %fusion.27, bf16[16,128,128]{2,1,0:T(8,128)(2,1)} %copy-done.16, bf16[384,2048]{1,0:T(8,128)(2,1)S(1)} %copy-done), kind=kOutput, calls=%fused_computation.17 | convolution fusion | flops 203685888 | bytes 9961472 | tf_op jit(solution)/shard_map/the,hde->thd/dot_general | solution.py:71
  290.7 1.6 copy.30
  (45 shorter events, 1.2 us)
Async XLA Ops:
  0.6 8.4 %copy-start = (bf16[384,2048]{1,0:T(8,128)(2,1)S(1)}, bf16[384,2048]{1,0:T(8,128)(2,1)}, u32[]{:S(2)}) copy-start(bf16[384,2048]{1,0:T(8,128)(2,1)} %param.7) | copy-start | bytes 4718596
  9.0 17.8 %copy-start.6 = (bf16[384,16,128]{0,2,1:T(8,128)(2,1)}, bf16[384,16,128]{0,2,1:T(8,128)(2,1)S(1)}, u32[]{:S(2)}) copy-start(bf16[384,16,128]{0,2,1:T(8,128)(2,1)S(1)} %copy.19) | copy-start | bytes 4718596
  9.6 43.4 %copy-start.11 = (f32[16,128,128]{2,1,0:T(8,128)}, f32[16,128,128]{2,1,0:T(8,128)S(1)}, u32[]{:S(2)}) copy-start(f32[16,128,128]{2,1,0:T(8,128)S(1)} %fusion.14) | copy-start | bytes 3145732
  9.6 17.0 %collective-permute-start = (f32[16,128,128]{2,1,0:T(8,128)S(1)}, f32[16,128,128]{2,1,0:T(8,128)S(1)}, u32[]{:S(2)}, u32[]{:S(2)}) collective-permute-start(f32[16,128,128]{2,1,0:T(8,128)S(1)} %fusion.14), channel_id=1, source_target_pairs={{0,1},{1,2},{2,3},{3,4},{4,5},{5,6},{6,7},{7,8},{8,9},{9,10},{10,1... | collective-permute-start | bytes 3145736 | tf_op jit(solution)/shard_map/ppermute | solution.py:14
  26.8 26.1 %collective-permute-start.1 = (f32[16,128,128]{2,1,0:T(8,128)S(1)}, f32[16,128,128]{2,1,0:T(8,128)S(1)}, u32[]{:S(2)}, u32[]{:S(2)}) collective-permute-start(f32[16,128,128]{2,1,0:T(8,128)S(1)} %add.66), channel_id=1, source_target_pairs={{0,2},{1,3},{2,4},{3,5},{4,6},{5,7},{6,8},{7,9},{8,10},{9,11},{10,... | collective-permute-start | bytes 3145736 | tf_op jit(solution)/shard_map/ppermute | solution.py:14
  53.0 27.0 %copy-start.17 = (bf16[384,2048]{1,0:T(8,128)(2,1)S(1)}, bf16[384,2048]{1,0:T(8,128)(2,1)}, u32[]{:S(2)}) copy-start(bf16[384,2048]{1,0:T(8,128)(2,1)} %param.5) | copy-start | bytes 4718596
  53.0 24.4 %collective-permute-start.2 = (f32[16,128,128]{2,1,0:T(8,128)S(1)}, f32[16,128,128]{2,1,0:T(8,128)S(1)}, u32[]{:S(2)}, u32[]{:S(2)}) collective-permute-start(f32[16,128,128]{2,1,0:T(8,128)S(1)} %add.67), channel_id=1, source_target_pairs={{0,4},{1,5},{2,6},{3,7},{4,8},{5,9},{6,10},{7,11},{8,12},{9,13},{1... | collective-permute-start | bytes 3145736 | tf_op jit(solution)/shard_map/ppermute | solution.py:14
  78.6 4.5 %copy-start.18 = (bf16[384,2048]{1,0:T(8,128)(2,1)S(1)}, bf16[384,2048]{1,0:T(8,128)(2,1)}, u32[]{:S(2)}) copy-start(bf16[384,2048]{1,0:T(8,128)(2,1)} %param.8) | copy-start | bytes 4718596
  78.6 24.8 %collective-permute-start.3 = (f32[16,128,128]{2,1,0:T(8,128)}, f32[16,128,128]{2,1,0:T(8,128)}, u32[]{:S(2)}, u32[]{:S(2)}) collective-permute-start(f32[16,128,128]{2,1,0:T(8,128)} %add.68), channel_id=1, source_target_pairs={{0,8},{1,9},{2,10},{3,11},{4,12},{5,13},{6,14},{7,15},{16,24},{17,... | collective-permute-start | bytes 3145736 | tf_op jit(solution)/shard_map/ppermute | solution.py:14
  90.2 2.1 copy-start.4
  90.2 13.1 %copy-start.12 = (f32[16,128,128]{2,1,0:T(8,128)S(1)}, f32[16,128,128]{2,1,0:T(8,128)}, u32[]{:S(2)}) copy-start(f32[16,128,128]{2,1,0:T(8,128)} %copy-done.11) | copy-start | bytes 3145732
  105.1 0.8 copy-start.14
  105.1 2.1 copy-start.1
  105.1 2.1 copy-start.19
  109.3 36.3 %copy-start.2 = (bf16[384,16,128]{0,2,1:T(8,128)(2,1)}, bf16[384,16,128]{0,2,1:T(8,128)(2,1)S(1)}, u32[]{:S(2)}) copy-start(bf16[384,16,128]{0,2,1:T(8,128)(2,1)S(1)} %divide_convert_fusion) | copy-start | bytes 4718596
  110.1 63.6 %copy-start.9 = (f32[16,128,128]{2,1,0:T(8,128)}, f32[16,128,128]{2,1,0:T(8,128)S(1)}, u32[]{:S(2)}) copy-start(f32[16,128,128]{2,1,0:T(8,128)S(1)} %fusion.28) | copy-start | bytes 3145732
  110.1 35.3 %collective-permute-start.4 = (f32[16,128,128]{2,1,0:T(8,128)S(1)}, f32[16,128,128]{2,1,0:T(8,128)S(1)}, u32[]{:S(2)}, u32[]{:S(2)}) collective-permute-start(f32[16,128,128]{2,1,0:T(8,128)S(1)} %fusion.28), channel_id=1, source_target_pairs={{1,0},{2,1},{3,2},{4,3},{5,4},{6,5},{7,6},{8,7},{9,8},{10,9},{11,1... | collective-permute-start | bytes 3145736 | tf_op jit(solution)/shard_map/ppermute | solution.py:14
  145.6 27.1 %collective-permute-start.5 = (f32[16,128,128]{2,1,0:T(8,128)S(1)}, f32[16,128,128]{2,1,0:T(8,128)S(1)}, u32[]{:S(2)}, u32[]{:S(2)}) collective-permute-start(f32[16,128,128]{2,1,0:T(8,128)S(1)} %add.75), channel_id=1, source_target_pairs={{2,0},{3,1},{4,2},{5,3},{6,4},{7,5},{8,6},{9,7},{10,8},{11,9},{12,... | collective-permute-start | bytes 3145736 | tf_op jit(solution)/shard_map/ppermute | solution.py:14
  173.7 28.2 %collective-permute-start.6 = (f32[16,128,128]{2,1,0:T(8,128)}, f32[16,128,128]{2,1,0:T(8,128)}, u32[]{:S(2)}, u32[]{:S(2)}) collective-permute-start(f32[16,128,128]{2,1,0:T(8,128)} %add.76), channel_id=1, source_target_pairs={{4,0},{5,1},{6,2},{7,3},{8,4},{9,5},{10,6},{11,7},{12,8},{13,9},{1... | collective-permute-start | bytes 3145736 | tf_op jit(solution)/shard_map/ppermute | solution.py:14
  183.7 3.2 %copy-start.7 = (bf16[384,16,128]{0,2,1:T(8,128)(2,1)S(1)}, bf16[384,16,128]{0,2,1:T(8,128)(2,1)}, u32[]{:S(2)}) copy-start(bf16[384,16,128]{0,2,1:T(8,128)(2,1)} %copy-done.6) | copy-start | bytes 4718596
  186.9 2.4 copy-start.5
  186.9 20.8 %copy-start.8 = (f32[384,2048]{0,1:T(8,128)S(1)}, f32[384,2048]{0,1:T(8,128)}, u32[]{:S(2)}) copy-start(f32[384,2048]{0,1:T(8,128)} %copy.21) | copy-start | bytes 9437188
  189.3 18.4 %copy-start.3 = (bf16[384,16,128]{0,2,1:T(8,128)(2,1)S(1)}, bf16[384,16,128]{0,2,1:T(8,128)(2,1)}, u32[]{:S(2)}) copy-start(bf16[384,16,128]{0,2,1:T(8,128)(2,1)} %copy-done.2) | copy-start | bytes 4718596
  189.3 18.4 %copy-start.15 = (bf16[16,128,128]{2,1,0:T(8,128)(2,1)S(1)}, bf16[16,128,128]{2,1,0:T(8,128)(2,1)}, u32[]{:S(2)}) copy-start(bf16[16,128,128]{2,1,0:T(8,128)(2,1)} %copy-done.14) | copy-start | bytes 1572868
  204.6 77.8 %collective-permute-start.7 = (f32[16,128,128]{2,1,0:T(8,128)}, f32[16,128,128]{2,1,0:T(8,128)}, u32[]{:S(2)}, u32[]{:S(2)}) collective-permute-start(f32[16,128,128]{2,1,0:T(8,128)} %add.77), channel_id=1, source_target_pairs={{8,0},{9,1},{10,2},{11,3},{12,4},{13,5},{14,6},{15,7},{24,16},{25,... | collective-permute-start | bytes 3145736 | tf_op jit(solution)/shard_map/ppermute | solution.py:14
  277.1 5.3 %copy-start.10 = (f32[16,128,128]{2,1,0:T(8,128)S(1)}, f32[16,128,128]{2,1,0:T(8,128)}, u32[]{:S(2)}) copy-start(f32[16,128,128]{2,1,0:T(8,128)} %copy-done.9) | copy-start | bytes 3145732
  282.4 2.0 copy-start.13
  284.5 0.8 copy-start.16
where the time goes:
time: 293 us; the launch traced here: 292 us
  waiting for transfers between devices  119 us (41%)
  blocking collectives  60.8 us (21%)
  starting transfers between devices  42.2 us (14%)
  matrix products  27.4 us (9%)
  local copies, waits for them, and re-layouts  23.4 us (8%)
  other arithmetic  18.8 us (6%)
    ppermute x8, waiting for transfers between devices, shifted(): lax.ppermute(value, axis, [(source, source + steps) for source in range(f...  119 us
    psum x1, blocking collectives, on_device(): gain_total = lax.psum(gain_part, 'seq')  60.8 us
    ppermute x8, starting transfers between devices, shifted(): lax.ppermute(value, axis, [(source, source + steps) for source in range(f...  42.2 us
    unnamed x44, local copies, waits for them, and re-layouts  10.2 us
    select_n x2, local copies, waits for them, and re-layouts, slope(): return jnp.where(x > 0, 1.0, jnp.exp(jnp.minimum(x, 0.0)))  7.07 us
  transfers between devices with their start and end apart: 8, of which 7 were waited for; matrix products, arithmetic and copies ran while one was open for 13% of the time, Pallas kernels for 0%

commit v1 on v0

--- a/solution.py
+++ b/solution.py
@@ -58,7 +58,13 @@
     for level in range(rounds):
         later = later + shifted(later, "seq", -(1 << level))
     back_low = (later - query_state).astype(jnp.bfloat16)
-    gain_total = lax.psum(gain_part, "seq")
+    devices = lax.axis_size("seq")
+    gain_total, reach = (gain_part, 1)
+    while reach < devices:
+        gain_total = gain_total + lax.ppermute(
+            gain_total, "seq", [(i, i ^ reach) for i in range(devices)]
+        )
+        reach = 2 * reach
     d_scores = jnp.einsum(
         "the,she->hts", grad_mixed, value_rows, preferred_element_type=jnp.float32
     )

time: 293 us -> 270 us (0.922); the launches traced: 292 us -> 265 us
  blocking collectives: 60.8 us -> 0 us
  waiting for transfers between devices: 119 us -> 151 us
  starting transfers between devices: 42.2 us -> 46.4 us
  matrix products: 27.4 us -> 23.9 us
    psum x1 -> x0, blocking collectives: 60.8 us -> none  [on_device(): gain_total = lax.psum(gain_part, 'seq')]
    ppermute x0 -> x4, waiting for transfers between devices: none -> 36.4 us  [on_device(): lax.ppermute(gain_total, 'seq', [(i, i ^ reach) for i in range(devices)])]
    ppermute x0 -> x4, starting transfers between devices: none -> 4.07 us  [on_device(): lax.ppermute(gain_total, 'seq', [(i, i ^ reach) for i in range(devices)])]
    ppermute x8, waiting for transfers between devices: 119 us -> 115 us  [shifted(): lax.ppermute(value, axis, [(source, source + steps) for source in range(f...]
    unnamed x44 -> x46, local copies, waits for them, and re-layouts: 10.2 us -> 9.42 us
  transfers between devices with their start and end apart: 8 -> 12, of which waited for: 7 -> 8; matrix products, arithmetic and copies ran while one was open for 13% -> 13% of each run, Pallas kernels for 0% -> 0%
where the time goes in v1:
time: 270 us; the launch traced here: 265 us
  waiting for transfers between devices  151 us (56%)
  starting transfers between devices  46.4 us (17%)
  matrix products  23.9 us (9%)
  local copies, waits for them, and re-layouts  22.8 us (8%)
  other arithmetic  19.5 us (7%)
    ppermute x8, waiting for transfers between devices, shifted(): lax.ppermute(value, axis, [(source, source + steps) for source in range(f...  115 us
    ppermute x8, starting transfers between devices, shifted(): lax.ppermute(value, axis, [(source, source + steps) for source in range(f...  42.3 us
    ppermute x4, waiting for transfers between devices, on_device(): lax.ppermute(gain_total, 'seq', [(i, i ^ reach) for i in range(devices)])  36.4 us
    unnamed x46, local copies, waits for them, and re-layouts  9.42 us
    select_n x2, local copies, waits for them, and re-layouts, slope(): return jnp.where(x > 0, 1.0, jnp.exp(jnp.minimum(x, 0.0)))  7.29 us
  transfers between devices with their start and end apart: 12, of which 8 were waited for; matrix products, arithmetic and copies ran while one was open for 13% of the time, Pallas kernels for 0%

profile of v1, /device:TPU:16, one launch (start us, length us, event | category | flops | bytes accessed | tf_op | source)
XLA Modules:
  0.0 264.7 jit_solution(8353340036778644456)
XLA Ops:
  0.6 4.9 %fusion.3 = (f32[384,2048]{1,0:T(8,128)}, bf16[48,16,8,128]{3,2,1,0:T(8,128)(2,1)}, bf16[48,8,16,128]{3,1,2,0:T(8,128)(2,1)S(1)}) fusion(bf16[384,2048]{1,0:T(8,128)(2,1)} %param.6), kind=kLoop, calls=%fused_computation.11 | loop fusion | flops 5505024 | bytes 7864320 | tf_op jit(solution)/shard_map/jit(_where)/select_n | solution.py:22
  5.5 1.6 copy.40
  7.1 2.1 copy.19
  9.8 1.9 collective-permute-start
  11.8 15.1 %collective-permute-done = f32[16,128,128]{2,1,0:T(8,128)S(1)} collective-permute-done((f32[16,128,128]{2,1,0:T(8,128)S(1)}, f32[16,128,128]{2,1,0:T(8,128)S(1)}, u32[]{:S(2)}, u32[]{:S(2)}) %collective-permute-start) | collective-permute-done | bytes 1048608 | tf_op jit(solution)/shard_map/ppermute | solution.py:14
  27.0 2.5 collective-permute-start.1
  29.5 23.6 %collective-permute-done.1 = f32[16,128,128]{2,1,0:T(8,128)S(1)} collective-permute-done((f32[16,128,128]{2,1,0:T(8,128)S(1)}, f32[16,128,128]{2,1,0:T(8,128)S(1)}, u32[]{:S(2)}, u32[]{:S(2)}) %collective-permute-start.1) | collective-permute-done | bytes 1048608 | tf_op jit(solution)/shard_map/ppermute | solution.py:14
  53.2 3.6 %collective-permute-start.2 = (f32[16,128,128]{2,1,0:T(8,128)S(1)}, f32[16,128,128]{2,1,0:T(8,128)S(1)}, u32[]{:S(2)}, u32[]{:S(2)}) collective-permute-start(f32[16,128,128]{2,1,0:T(8,128)S(1)} %add.77), channel_id=1, source_target_pairs={{0,4},{1,5},{2,6},{3,7},{4,8},{5,9},{6,10},{7,11},{8,12},{9,13},{1... | collective-permute-start | bytes 3145736 | tf_op jit(solution)/shard_map/ppermute | solution.py:14
  56.9 20.8 %collective-permute-done.2 = f32[16,128,128]{2,1,0:T(8,128)S(1)} collective-permute-done((f32[16,128,128]{2,1,0:T(8,128)S(1)}, f32[16,128,128]{2,1,0:T(8,128)S(1)}, u32[]{:S(2)}, u32[]{:S(2)}) %collective-permute-start.2) | collective-permute-done | bytes 1048608 | tf_op jit(solution)/shard_map/ppermute | solution.py:14
  77.6 1.1 add.78
  78.8 1.4 collective-permute-start.3
  80.2 3.1 %fusion.5 = (bf16[384,2048]{1,0:T(8,128)(2,1)}, f32[384,2048]{1,0:T(8,128)}) fusion(bf16[384,2048]{1,0:T(8,128)(2,1)S(1)} %copy-done.16), kind=kLoop, calls=%fused_computation.13 | loop fusion | flops 5505024 | bytes 6291456 | tf_op jit(solution)/shard_map/convert.1
  83.3 2.1 copy.9
  85.4 1.9 copy.37
  87.3 3.1 %select_convert_fusion.1 = bf16[16,384,384]{2,1,0:T(8,128)(2,1)S(1)} fusion(pred[384,384]{1,0:T(8,128)(4,1)S(1)} %iota_compare_fusion, bf16[384,16,128]{0,2,1:T(8,128)(2,1)S(1)} %bitcast.77, bf16[48,16,8,128]{3,2,1,0:T(8,128)(2,1)} %get-tuple-element.11), kind=kOutput, calls=%fused_computation.1 | convolution fusion | flops 608698368 | bytes 8011776 | tf_op jit(solution)/shard_map/thd,shd->hts/dot_general | solution.py:41
  90.4 1.6 fusion.10
  92.6 11.0 %collective-permute-done.3 = f32[16,128,128]{2,1,0:T(8,128)} collective-permute-done((f32[16,128,128]{2,1,0:T(8,128)}, f32[16,128,128]{2,1,0:T(8,128)}, u32[]{:S(2)}, u32[]{:S(2)}) %collective-permute-start.3) | collective-permute-done | bytes 1048608 | tf_op jit(solution)/shard_map/ppermute | solution.py:14
  103.5 1.8 subtract_convert_fusion.1
  106.1 1.3 copy-done.1
  107.4 1.3 multiply_reduce_fusion
  108.7 0.8 divide_convert_fusion
  109.5 0.8 fusion.28
  110.3 23.0 %collective-permute-start.4 = (f32[16,128,128]{2,1,0:T(8,128)S(1)}, f32[16,128,128]{2,1,0:T(8,128)S(1)}, u32[]{:S(2)}, u32[]{:S(2)}) collective-permute-start(f32[16,128,128]{2,1,0:T(8,128)S(1)} %fusion.28), channel_id=1, source_target_pairs={{1,0},{2,1},{3,2},{4,3},{5,4},{6,5},{7,6},{8,7},{9,8},{10,9},{11,1... | collective-permute-start | bytes 3145736 | tf_op jit(solution)/shard_map/ppermute | solution.py:14
  133.3 12.3 %collective-permute-done.4 = f32[16,128,128]{2,1,0:T(8,128)S(1)} collective-permute-done((f32[16,128,128]{2,1,0:T(8,128)S(1)}, f32[16,128,128]{2,1,0:T(8,128)S(1)}, u32[]{:S(2)}, u32[]{:S(2)}) %collective-permute-start.4) | collective-permute-done | bytes 1048608 | tf_op jit(solution)/shard_map/ppermute | solution.py:14
  145.6 1.1 add.85
  146.8 4.0 %collective-permute-start.5 = (f32[16,128,128]{2,1,0:T(8,128)}, f32[16,128,128]{2,1,0:T(8,128)}, u32[]{:S(2)}, u32[]{:S(2)}) collective-permute-start(f32[16,128,128]{2,1,0:T(8,128)} %add.85), channel_id=1, source_target_pairs={{2,0},{3,1},{4,2},{5,3},{6,4},{7,5},{8,6},{9,7},{10,8},{11,9},{12,... | collective-permute-start | bytes 3145736 | tf_op jit(solution)/shard_map/ppermute | solution.py:14
  150.8 3.6 %copy.21 = f32[384,2048]{0,1:T(8,128)} copy(f32[384,2048]{1,0:T(8,128)} %get-tuple-element.14) | data formatting | bytes 6291456 | tf_op jit(solution)/shard_map/jit(_where)/select_n | solution.py:22
  154.4 3.7 %copy.26 = f32[384,2048]{0,1:T(8,128)} copy(f32[384,2048]{1,0:T(8,128)} %get-tuple-element.10) | data formatting | bytes 6291456 | tf_op jit(solution)/shard_map/jit(_where)/select_n | solution.py:22
  158.1 16.1 %collective-permute-done.5 = f32[16,128,128]{2,1,0:T(8,128)} collective-permute-done((f32[16,128,128]{2,1,0:T(8,128)}, f32[16,128,128]{2,1,0:T(8,128)}, u32[]{:S(2)}, u32[]{:S(2)}) %collective-permute-start.5) | collective-permute-done | bytes 1048608 | tf_op jit(solution)/shard_map/ppermute | solution.py:14
  174.1 1.7 add.86
  175.8 2.8 %collective-permute-start.6 = (f32[16,128,128]{2,1,0:T(8,128)S(1)}, f32[16,128,128]{2,1,0:T(8,128)S(1)}, u32[]{:S(2)}, u32[]{:S(2)}) collective-permute-start(f32[16,128,128]{2,1,0:T(8,128)S(1)} %add.86), channel_id=1, source_target_pairs={{4,0},{5,1},{6,2},{7,3},{8,4},{9,5},{10,6},{11,7},{12,8},{13,9},{1... | collective-permute-start | bytes 3145736 | tf_op jit(solution)/shard_map/ppermute | solution.py:14
  178.7 1.7 select_convert_fusion
  181.0 1.6 fusion.26
  182.6 2.8 %collective-permute-start.9 = (f32[16,128]{1,0:T(8,128)S(1)}, f32[16,128]{1,0:T(8,128)S(1)}, u32[]{:S(2)}, u32[]{:S(2)}) collective-permute-start(f32[16,128]{1,0:T(8,128)S(1)} %add.92), channel_id=1, source_target_pairs={{0,2},{1,3},{2,0},{3,1},{4,6},{5,7},{6,4},{7,5},{8,10},{9,11},{10,... | collective-permute-start | bytes 24584 | tf_op jit(solution)/shard_map/ppermute | solution.py:64
  185.3 1.9 fusion.9
  187.3 0.7 collective-permute-start.10
  188.0 15.9 %collective-permute-done.6 = f32[16,128,128]{2,1,0:T(8,128)S(1)} collective-permute-done((f32[16,128,128]{2,1,0:T(8,128)S(1)}, f32[16,128,128]{2,1,0:T(8,128)S(1)}, u32[]{:S(2)}, u32[]{:S(2)}) %collective-permute-start.6) | collective-permute-done | bytes 1048608 | tf_op jit(solution)/shard_map/ppermute | solution.py:14
  203.9 1.1 add.87
  205.0 3.0 %collective-permute-start.7 = (f32[16,128,128]{2,1,0:T(8,128)}, f32[16,128,128]{2,1,0:T(8,128)}, u32[]{:S(2)}, u32[]{:S(2)}) collective-permute-start(f32[16,128,128]{2,1,0:T(8,128)} %add.87), channel_id=1, source_target_pairs={{8,0},{9,1},{10,2},{11,3},{12,4},{13,5},{14,6},{15,7},{24,16},{25,... | collective-permute-start | bytes 3145736 | tf_op jit(solution)/shard_map/ppermute | solution.py:14
  208.0 2.9 %fusion.29 = f32[16,128,384]{2,1,0:T(8,128)} fusion(bf16[384,16,128]{0,2,1:T(8,128)(2,1)S(1)} %copy-done.3, bf16[16,384,384]{2,1,0:T(8,128)(2,1)S(1)} %bitcast.82), kind=kOutput, calls=%fused_computation.52 | convolution fusion | flops 603979776 | bytes 9437184 | tf_op jit(solution)/shard_map/hts,the->she/dot_general | solution.py:80
  210.9 2.9 %fusion.27 = f32[16,128,384]{2,1,0:T(8,128)} fusion(bf16[384,16,128]{0,2,1:T(8,128)(2,1)S(1)} %bitcast.80, bf16[16,384,384]{2,1,0:T(8,128)(2,1)S(1)} %select_convert_fusion), kind=kOutput, calls=%fused_computation.50 | convolution fusion | flops 603979776 | bytes 9437184 | tf_op jit(solution)/shard_map/hts,thd->shd/dot_general | solution.py:76
  213.8 2.7 %copy.29 = bf16[384,2048]{1,0:T(8,128)(2,1)} copy(bf16[384,2048]{0,1:T(8,128)(2,1)} %bitcast.85) | data formatting | bytes 3145728
  216.5 36.4 %collective-permute-done.11 = f32[16,128]{1,0:T(8,128)S(1)} collective-permute-done((f32[16,128]{1,0:T(8,128)S(1)}, f32[16,128]{1,0:T(8,128)S(1)}, u32[]{:S(2)}, u32[]{:S(2)}) %collective-permute-start.11) | collective-permute-done | bytes 8224 | tf_op jit(solution)/shard_map/ppermute | solution.py:64
  253.5 1.7 subtract_convert_fusion
  255.2 2.4 add_convert_fusion
  257.7 1.6 copy.31
  259.3 3.8 %fusion.8 = bf16[384,16,128]{0,2,1:T(8,128)(2,1)S(1)} fusion(f32[384,16,128]{0,2,1:T(8,128)} %bitcast.83, f32[16,128,384]{2,1,0:T(8,128)} %fusion.27, bf16[16,128,128]{2,1,0:T(8,128)(2,1)} %copy-done.15, bf16[384,2048]{1,0:T(8,128)(2,1)S(1)} %copy-done), kind=kOutput, calls=%fused_computation.17 | convolution fusion | flops 203685888 | bytes 9961472 | tf_op jit(solution)/shard_map/the,hde->thd/dot_general | solution.py:77
  263.1 1.6 copy.30
  (59 shorter events, 3.4 us)
Async XLA Ops:
  0.6 8.6 %copy-start = (bf16[384,2048]{1,0:T(8,128)(2,1)S(1)}, bf16[384,2048]{1,0:T(8,128)(2,1)}, u32[]{:S(2)}) copy-start(bf16[384,2048]{1,0:T(8,128)(2,1)} %param.7) | copy-start | bytes 4718596
  9.2 17.7 %copy-start.5 = (bf16[384,16,128]{0,2,1:T(8,128)(2,1)}, bf16[384,16,128]{0,2,1:T(8,128)(2,1)S(1)}, u32[]{:S(2)}) copy-start(bf16[384,16,128]{0,2,1:T(8,128)(2,1)S(1)} %copy.19) | copy-start | bytes 4718596
  9.8 43.4 %copy-start.11 = (f32[16,128,128]{2,1,0:T(8,128)}, f32[16,128,128]{2,1,0:T(8,128)S(1)}, u32[]{:S(2)}) copy-start(f32[16,128,128]{2,1,0:T(8,128)S(1)} %fusion.14) | copy-start | bytes 3145732
  9.8 17.0 %collective-permute-start = (f32[16,128,128]{2,1,0:T(8,128)S(1)}, f32[16,128,128]{2,1,0:T(8,128)S(1)}, u32[]{:S(2)}, u32[]{:S(2)}) collective-permute-start(f32[16,128,128]{2,1,0:T(8,128)S(1)} %fusion.14), channel_id=1, source_target_pairs={{0,1},{1,2},{2,3},{3,4},{4,5},{5,6},{6,7},{7,8},{8,9},{9,10},{10,1... | collective-permute-start | bytes 3145736 | tf_op jit(solution)/shard_map/ppermute | solution.py:14
  27.0 26.1 %collective-permute-start.1 = (f32[16,128,128]{2,1,0:T(8,128)S(1)}, f32[16,128,128]{2,1,0:T(8,128)S(1)}, u32[]{:S(2)}, u32[]{:S(2)}) collective-permute-start(f32[16,128,128]{2,1,0:T(8,128)S(1)} %add.76), channel_id=1, source_target_pairs={{0,2},{1,3},{2,4},{3,5},{4,6},{5,7},{6,8},{7,9},{8,10},{9,11},{10,... | collective-permute-start | bytes 3145736 | tf_op jit(solution)/shard_map/ppermute | solution.py:14
  53.2 26.9 %copy-start.16 = (bf16[384,2048]{1,0:T(8,128)(2,1)S(1)}, bf16[384,2048]{1,0:T(8,128)(2,1)}, u32[]{:S(2)}) copy-start(bf16[384,2048]{1,0:T(8,128)(2,1)} %param.5) | copy-start | bytes 4718596
  53.2 24.4 %collective-permute-start.2 = (f32[16,128,128]{2,1,0:T(8,128)S(1)}, f32[16,128,128]{2,1,0:T(8,128)S(1)}, u32[]{:S(2)}, u32[]{:S(2)}) collective-permute-start(f32[16,128,128]{2,1,0:T(8,128)S(1)} %add.77), channel_id=1, source_target_pairs={{0,4},{1,5},{2,6},{3,7},{4,8},{5,9},{6,10},{7,11},{8,12},{9,13},{1... | collective-permute-start | bytes 3145736 | tf_op jit(solution)/shard_map/ppermute | solution.py:14
  78.8 4.5 %copy-start.17 = (bf16[384,2048]{1,0:T(8,128)(2,1)S(1)}, bf16[384,2048]{1,0:T(8,128)(2,1)}, u32[]{:S(2)}) copy-start(bf16[384,2048]{1,0:T(8,128)(2,1)} %param.8) | copy-start | bytes 4718596
  78.8 24.8 %collective-permute-start.3 = (f32[16,128,128]{2,1,0:T(8,128)}, f32[16,128,128]{2,1,0:T(8,128)}, u32[]{:S(2)}, u32[]{:S(2)}) collective-permute-start(f32[16,128,128]{2,1,0:T(8,128)} %add.78), channel_id=1, source_target_pairs={{0,8},{1,9},{2,10},{3,11},{4,12},{5,13},{6,14},{7,15},{16,24},{17,... | collective-permute-start | bytes 3145736 | tf_op jit(solution)/shard_map/ppermute | solution.py:14
  90.4 2.2 copy-start.4
  90.4 13.1 %copy-start.12 = (f32[16,128,128]{2,1,0:T(8,128)S(1)}, f32[16,128,128]{2,1,0:T(8,128)}, u32[]{:S(2)}) copy-start(f32[16,128,128]{2,1,0:T(8,128)} %copy-done.11) | copy-start | bytes 3145732
  105.3 0.8 copy-start.13
  105.3 2.1 copy-start.1
  105.3 2.1 copy-start.18
  109.5 37.2 %copy-start.2 = (bf16[384,16,128]{0,2,1:T(8,128)(2,1)}, bf16[384,16,128]{0,2,1:T(8,128)(2,1)S(1)}, u32[]{:S(2)}) copy-start(bf16[384,16,128]{0,2,1:T(8,128)(2,1)S(1)} %divide_convert_fusion) | copy-start | bytes 4718596
  110.3 40.5 %copy-start.9 = (f32[16,128,128]{2,1,0:T(8,128)}, f32[16,128,128]{2,1,0:T(8,128)S(1)}, u32[]{:S(2)}) copy-start(f32[16,128,128]{2,1,0:T(8,128)S(1)} %fusion.28) | copy-start | bytes 3145732
  110.3 35.3 %collective-permute-start.4 = (f32[16,128,128]{2,1,0:T(8,128)S(1)}, f32[16,128,128]{2,1,0:T(8,128)S(1)}, u32[]{:S(2)}, u32[]{:S(2)}) collective-permute-start(f32[16,128,128]{2,1,0:T(8,128)S(1)} %fusion.28), channel_id=1, source_target_pairs={{1,0},{2,1},{3,2},{4,3},{5,4},{6,5},{7,6},{8,7},{9,8},{10,9},{11,1... | collective-permute-start | bytes 3145736 | tf_op jit(solution)/shard_map/ppermute | solution.py:14
  146.8 27.4 %collective-permute-start.5 = (f32[16,128,128]{2,1,0:T(8,128)}, f32[16,128,128]{2,1,0:T(8,128)}, u32[]{:S(2)}, u32[]{:S(2)}) collective-permute-start(f32[16,128,128]{2,1,0:T(8,128)} %add.85), channel_id=1, source_target_pairs={{2,0},{3,1},{4,2},{5,3},{6,4},{7,5},{8,6},{9,7},{10,8},{11,9},{12,... | collective-permute-start | bytes 3145736 | tf_op jit(solution)/shard_map/ppermute | solution.py:14
  158.1 20.6 %copy-start.3 = (bf16[384,16,128]{0,2,1:T(8,128)(2,1)S(1)}, bf16[384,16,128]{0,2,1:T(8,128)(2,1)}, u32[]{:S(2)}) copy-start(bf16[384,16,128]{0,2,1:T(8,128)(2,1)} %copy-done.2) | copy-start | bytes 4718596
  175.8 5.1 %copy-start.6 = (bf16[384,16,128]{0,2,1:T(8,128)(2,1)S(1)}, bf16[384,16,128]{0,2,1:T(8,128)(2,1)}, u32[]{:S(2)}) copy-start(bf16[384,16,128]{0,2,1:T(8,128)(2,1)} %copy-done.5) | copy-start | bytes 4718596
  175.8 28.1 %collective-permute-start.6 = (f32[16,128,128]{2,1,0:T(8,128)S(1)}, f32[16,128,128]{2,1,0:T(8,128)S(1)}, u32[]{:S(2)}, u32[]{:S(2)}) collective-permute-start(f32[16,128,128]{2,1,0:T(8,128)S(1)} %add.86), channel_id=1, source_target_pairs={{4,0},{5,1},{6,2},{7,3},{8,4},{9,5},{10,6},{11,7},{12,8},{13,9},{1... | collective-permute-start | bytes 3145736 | tf_op jit(solution)/shard_map/ppermute | solution.py:14
  180.4 4.9 %copy-start.7 = (f32[384,2048]{0,1:T(8,128)S(1)}, f32[384,2048]{0,1:T(8,128)}, u32[]{:S(2)}) copy-start(f32[384,2048]{0,1:T(8,128)} %copy.21) | copy-start | bytes 9437188
  180.4 4.9 %copy-start.14 = (bf16[16,128,128]{2,1,0:T(8,128)(2,1)S(1)}, bf16[16,128,128]{2,1,0:T(8,128)(2,1)}, u32[]{:S(2)}) copy-start(bf16[16,128,128]{2,1,0:T(8,128)(2,1)} %copy-done.13) | copy-start | bytes 1572868
  180.4 2.1 collective-permute-start.8
  182.6 4.7 %collective-permute-start.9 = (f32[16,128]{1,0:T(8,128)S(1)}, f32[16,128]{1,0:T(8,128)S(1)}, u32[]{:S(2)}, u32[]{:S(2)}) collective-permute-start(f32[16,128]{1,0:T(8,128)S(1)} %add.92), channel_id=1, source_target_pairs={{0,2},{1,3},{2,0},{3,1},{4,6},{5,7},{6,4},{7,5},{8,10},{9,11},{10,... | collective-permute-start | bytes 24584 | tf_op jit(solution)/shard_map/ppermute | solution.py:64
  185.3 22.7 %slice-start = ((s8[4718592]{0:T(1024)(128)(4,1)}), s8[4194304]{0:T(1024)(128)(4,1)S(1)}, s32[]{:S(2)}) async-start(s8[4718592]{0:T(1024)(128)(4,1)} %bitcast.81), calls=%async_computation | async-start | bytes 8388608
  185.3 22.7 %slice-start.1 = ((s8[4718592]{0:T(1024)(128)(4,1)}), s8[524288]{0:T(1024)(128)(4,1)S(1)}, s32[]{:S(2)}) async-start(s8[4718592]{0:T(1024)(128)(4,1)} %bitcast.81), calls=%async_computation.1 | async-start | bytes 1048576
  187.3 23.6 %collective-permute-start.10 = (f32[16,128]{1,0:T(8,128)S(1)}, f32[16,128]{1,0:T(8,128)S(1)}, u32[]{:S(2)}, u32[]{:S(2)}) collective-permute-start(f32[16,128]{1,0:T(8,128)S(1)} %add.93), channel_id=1, source_target_pairs={{0,4},{1,5},{2,6},{3,7},{4,0},{5,1},{6,2},{7,3},{8,12},{9,13},{10,... | collective-permute-start | bytes 24584 | tf_op jit(solution)/shard_map/ppermute | solution.py:64
  205.0 48.5 %collective-permute-start.7 = (f32[16,128,128]{2,1,0:T(8,128)}, f32[16,128,128]{2,1,0:T(8,128)}, u32[]{:S(2)}, u32[]{:S(2)}) collective-permute-start(f32[16,128,128]{2,1,0:T(8,128)} %add.87), channel_id=1, source_target_pairs={{8,0},{9,1},{10,2},{11,3},{12,4},{13,5},{14,6},{15,7},{24,16},{25,... | collective-permute-start | bytes 3145736 | tf_op jit(solution)/shard_map/ppermute | solution.py:14
  210.9 42.0 %collective-permute-start.11 = (f32[16,128]{1,0:T(8,128)S(1)}, f32[16,128]{1,0:T(8,128)S(1)}, u32[]{:S(2)}, u32[]{:S(2)}) collective-permute-start(f32[16,128]{1,0:T(8,128)S(1)} %add.94), channel_id=1, source_target_pairs={{0,8},{1,9},{2,10},{3,11},{4,12},{5,13},{6,14},{7,15},{8,0},{9,1},... | collective-permute-start | bytes 24584 | tf_op jit(solution)/shard_map/ppermute | solution.py:64
  213.8 39.7 %copy-start.10 = (f32[16,128,128]{2,1,0:T(8,128)S(1)}, f32[16,128,128]{2,1,0:T(8,128)}, u32[]{:S(2)}) copy-start(f32[16,128,128]{2,1,0:T(8,128)} %copy-done.9) | copy-start | bytes 3145732
  216.5 38.8 %copy-start.8 = (f32[16,128,384]{2,1,0:T(8,128)S(1)}, f32[16,128,384]{2,1,0:T(8,128)}, u32[]{:S(2)}) copy-start(f32[16,128,384]{2,1,0:T(8,128)} %fusion.29) | copy-start | bytes 9437188
  255.2 2.4 copy-start.15
